TPU v7x, 256 devices: a whole 4x4x8 slice. The times are simulated.
256 devices in a mesh: row: 16 (over y_lo, z), col: 16 (over y_hi, x, core).
Axes of the slice: x: 4, y: 4 (y_hi: 2, y_lo: 2; y = y_hi * 2 + y_lo), z: 8, core: 2. Of those that a mesh axis runs over, the one named last changes fastest.
Arguments:
- early_coords: bfloat16 [64, 32768], P(None, ('row', 'col')), may hold values from -13 to 13
- late_coords: bfloat16 [64, 131072], P(None, ('row', 'col')), may hold values from -13 to 13
- late_log_scale: bfloat16 [131072], P(('row', 'col')), may hold values from -2 to 115
- fate_labels: int32 [32768], P(('row', 'col')), may hold values from 0 to 255, as said below
- loadings: float32 [64, 2000], replicated, may hold values from -0.75 to 0.75
Outputs:
- projected: float32 [64, 32768], P(None, ('row', 'col'))
- fate_corr: float32 [2000, 256], replicated
Inputs may be any that keep to these rules, and one draw needn't show every extreme that they name: `fate_labels`: every one of the 256 fate classes labels at least one early cell.
All inputs are finite; a program needn't handle non-finite values.
Results may differ from a plain program's by a relative error of at most 0.0003.
Values may be sent and summed in bfloat16 or wider, within the bound.
No kernel may reach another device: no remote copies, remote signals or barrier semaphores. Data moves between devices by JAX's collectives and lax.ppermute only.
A program may use at most 64 MiB of HBM per device.

v0:
```python
import math
import jax
import jax.numpy as jnp
from jax import lax
from jax.sharding import PartitionSpec as P

FATES = 256
kernel_ratio = 8.0
epsilon = 1e-06


def per_device(early_coords, late_coords, late_log_scale, fate_labels, loadings):
    precise = lax.Precision.HIGHEST
    coord_dim = early_coords.shape[0]
    own_cells = early_coords.shape[1]
    early_rows = lax.all_gather(early_coords, "col", axis=1, tiled=True)
    late_rows, late_logs = (
        lax.all_gather(late_coords, "row", axis=1, tiled=True),
        lax.all_gather(late_log_scale, "row", axis=0, tiled=True),
    )
    sharpness = kernel_ratio / coord_dim
    late_wide = late_rows.astype(jnp.float32)
    late_norms = jnp.sum(late_wide * late_wide, 0)
    log_weights = late_logs.astype(jnp.float32)
    block_total = early_rows.shape[1]
    stride = math.gcd(block_total, 512)
    blocks = block_total // stride
    col_count = lax.axis_size("col")

    def scores_at(first_row):
        row_slab = lax.dynamic_slice_in_dim(early_rows, first_row, stride, 1)
        crossed = lax.dot_general(
            row_slab, late_rows, (((0,), (0,)), ((), ())), preferred_element_type=jnp.float32
        )
        slab_wide = row_slab.astype(jnp.float32)
        slab_norms = jnp.sum(slab_wide * slab_wide, 0)
        distance = slab_norms[:, None] + late_norms[None, :] - 2.0 * crossed
        return log_weights[None, :] - distance * sharpness

    def accumulate(first_row, scores, row_top, carried):
        numerators, totals = carried
        kernel = jnp.exp(scores - row_top[:, None])
        row_sums = jnp.sum(kernel, 1)
        partial_num = lax.dot_general(
            late_wide, kernel, (((1,), (1,)), ((), ())), precision=precise
        )
        numerators = lax.dynamic_update_slice_in_dim(numerators, partial_num, first_row, 1)
        totals = lax.dynamic_update_slice_in_dim(totals, row_sums, first_row, 0)
        return (numerators, totals)

    start_state = (
        jnp.zeros((coord_dim, block_total), jnp.float32),
        jnp.zeros((block_total,), jnp.float32),
    )

    def advance(block_index, carried):
        first_row = block_index * stride
        scores = scores_at(first_row)
        row_top = lax.pmax(jnp.max(scores, 1), "col")
        return accumulate(first_row, scores, row_top, carried)

    numerators, totals = lax.fori_loop(0, blocks, advance, start_state)
    own_num, own_total = (
        lax.psum_scatter(numerators, "col", scatter_dimension=1, tiled=True),
        lax.psum_scatter(totals, "col", scatter_dimension=0, tiled=True),
    )
    projected = own_num / own_total[None, :]
    displacement = projected - early_coords.astype(jnp.float32)
    classes = lax.broadcasted_iota(jnp.int32, (FATES, own_cells), 0)
    indicator = (fate_labels[None, :] == classes).astype(jnp.float32)
    fate_count = jnp.sum(indicator, 1)
    gene_shift = lax.dot_general(
        loadings, displacement, (((0,), (0,)), ((), ())), precision=precise
    )
    cross_sum = lax.dot_general(gene_shift, indicator, (((1,), (1,)), ((), ())), precision=precise)
    gene_total = jnp.sum(gene_shift, 1)
    gene_square = jnp.sum(gene_shift * gene_shift, 1)
    cross_sum, gene_total, gene_square, fate_count = lax.psum(
        (cross_sum, gene_total, gene_square, fate_count), ("row", "col")
    )
    cell_count = float(own_cells * lax.axis_size("row") * col_count)
    mean_shift = gene_total / cell_count
    variance = gene_square / cell_count - mean_shift * mean_shift + epsilon
    fate_share = fate_count / cell_count
    spread = fate_share * (1.0 - fate_share)
    covariance = cross_sum / cell_count - mean_shift[:, None] * fate_share[None, :]
    fate_corr = covariance / jnp.sqrt(variance[:, None] * spread[None, :])
    return (projected, fate_corr)


def solution(mesh):
    in_specs = (
        P(None, ("row", "col")),
        P(None, ("row", "col")),
        P(("row", "col")),
        P(("row", "col")),
        P(),
    )
    out_specs = (P(None, ("row", "col")), P())
    return jax.shard_map(
        per_device, mesh=mesh, in_specs=in_specs, out_specs=out_specs, check_vma=False
    )
```

profile of v0, /device:TPU:2, one launch (start us, length us, event | category | flops | bytes accessed | tf_op | source)
XLA Modules:
  0.0 715.3 jit_solution(15114682783649457366)
XLA Ops:
  7.2 0.0 copy-start
  7.2 0.0 all-gather.3.cloned.1.call-start
  7.2 0.7 all-gather.3.cloned.1.call-update
  7.9 0.0 reduce-scatter.2.cloned.1.call-start
  8.0 0.7 reshape.14
  8.6 36.5 %all-gather = bf16[16,1,512]{2,1,0:T(2,128)(2,1)S(1)} all-gather(bf16[1,1,512]{2,1,0:T(2,128)(2,1)S(1)} %reshape.14), channel_id=1, replica_groups=mesh['row'=16,'col'=16] {'row'}, dimensions={0}, use_global_device_ids=true | all-gather | bytes 17408 | tf_op jit(solution)/shard_map/all_gather | solution.py:19
  45.2 20.9 %all_gather.10 = bf16[64,2048]{1,0:T(8,128)(2,1)S(1)} all-gather(bf16[64,128]{1,0:T(8,128)(2,1)} %param.7), channel_id=1, replica_groups=mesh['row'=16,'col'=16] {'col'}, dimensions={1}, use_global_device_ids=true | all-gather | bytes 278528 | tf_op jit(solution)/shard_map/all_gather | solution.py:16
  66.1 15.7 %all-gather.3.cloned.1.call-done = bf16[64,8192]{1,0:T(8,128)(2,1)} async-done(((bf16[64,512]{1,0:T(8,128)(2,1)}), bf16[64,8192]{1,0:T(8,128)(2,1)}) %all-gather.3.cloned.1.call-update) | async-done | bytes 1048592 | tf_op jit(solution)/shard_map/all_gather | solution.py:18
  81.8 1.4 convert_element_type.20
  83.2 1.5 multiply_reduce_fusion.1
  84.7 0.0 copy-start.5
  84.7 0.0 copy-start.3
  84.8 0.0 copy-start.4
  84.8 276.3 %while.15 = (s32[]{:T(128)}, f32[64,2048]{1,0:T(8,128)S(1)}, f32[2048]{0:T(1024)S(1)}, f32[8192]{0:T(1024)S(1)}, bf16[64,2048]{1,0:T(8,128)(2,1)S(1)}, /*index=5...) while((s32[]{:T(128)}, f32[64,2048]{1,0:T(8,128)S(1)}, ...), condition=%wide.region_6.0_spmd, body=%wide.region_1.0_spmd.sunk | while | flops 3795942400 | bytes 53825716 | solution.py:62
  84.8 9.2 %fusion.25 = (f32[512]{0:T(512)S(1)}, f32[512,8192]{1,0:T(8,128)}) fusion(bf16[64,8192]{1,0:T(8,128)(2,1)} %get-tuple-element.255, bf16[64,2048]{1,0:T(8,128)(2,1)S(1)} %get-tuple-element.253, s32[]{:T(128)S(6)} %select_n.10, f32[8192]{0:T(1024)S(1)} %get-tuple-element.254, f32[512]{0:T(512)S(1)} %multiply_reduce_fusion.4, ...), kind=kOutput, calls=%fused_computation.26.clone.1 | convolution fusion | flops 562036224 | bytes 17960964 | tf_op jit(solution)/shard_map/while/body/eval_jaxpr/dot_general | solution.py:32
  94.0 27.9 %pmax.12 = f32[512]{0:T(512)S(1)} all-reduce(f32[512]{0:T(512)S(1)} %get-tuple-element.224), channel_id=1, replica_groups=mesh['row'=16,'col'=16] {'col'}, use_global_device_ids=true, to_apply=%region_4.0 | all-reduce | flops 512 | bytes 4096 | tf_op jit(solution)/shard_map/while/body/eval_jaxpr/pmax | solution.py:59
  122.0 8.1 %fusion.27 = f32[512]{0:T(512)S(1)} fusion(f32[512,8192]{1,0:T(8,128)} %get-tuple-element.223, f32[512]{0:T(512)S(1)} %pmax.12), kind=kLoop, calls=%fused_computation.2.clone.1 | loop fusion | flops 8388096 | bytes 16781312 | tf_op jit(solution)/shard_map/while/body/eval_jaxpr/reduce_sum | solution.py:43
  130.1 0.3 dynamic_update_slice.18
  130.4 19.6 %fusion.26 = f32[64,2048]{1,0:T(8,128)S(1)} fusion(f32[64,2048]{1,0:T(8,128)S(1)} %get-tuple-element.238, s32[]{:T(128)S(6)} %select_n.10, f32[64,8192]{1,0:T(8,128)S(1)} %get-tuple-element.256, f32[512,8192]{1,0:T(8,128)} %get-tuple-element.223, f32[512]{0:T(512)S(1)} %pmax.12), kind=kOutput, calls=%fused_computation.6.clone.1 | convolution fusion | flops 3225419776 | bytes 19007492 | tf_op jit(solution)/shard_map/while/body/eval_jaxpr/dot_general | solution.py:44
  150.0 9.2 %fusion.25 = (f32[512]{0:T(512)S(1)}, f32[512,8192]{1,0:T(8,128)}) fusion(bf16[64,8192]{1,0:T(8,128)(2,1)} %get-tuple-element.255, bf16[64,2048]{1,0:T(8,128)(2,1)S(1)} %get-tuple-element.253, s32[]{:T(128)S(6)} %select_n.10, f32[8192]{0:T(1024)S(1)} %get-tuple-element.254, f32[512]{0:T(512)S(1)} %multiply_reduce_fusion.4, ...), kind=kOutput, calls=%fused_computation.26.clone.1 | convolution fusion | flops 562036224 | bytes 17960964 | tf_op jit(solution)/shard_map/while/body/eval_jaxpr/dot_general | solution.py:32
  159.2 33.1 %pmax.12 = f32[512]{0:T(512)S(1)} all-reduce(f32[512]{0:T(512)S(1)} %get-tuple-element.224), channel_id=1, replica_groups=mesh['row'=16,'col'=16] {'col'}, use_global_device_ids=true, to_apply=%region_4.0 | all-reduce | flops 512 | bytes 4096 | tf_op jit(solution)/shard_map/while/body/eval_jaxpr/pmax | solution.py:59
  192.4 8.1 %fusion.27 = f32[512]{0:T(512)S(1)} fusion(f32[512,8192]{1,0:T(8,128)} %get-tuple-element.223, f32[512]{0:T(512)S(1)} %pmax.12), kind=kLoop, calls=%fused_computation.2.clone.1 | loop fusion | flops 8388096 | bytes 16781312 | tf_op jit(solution)/shard_map/while/body/eval_jaxpr/reduce_sum | solution.py:43
  200.5 0.3 dynamic_update_slice.18
  200.8 19.6 %fusion.26 = f32[64,2048]{1,0:T(8,128)S(1)} fusion(f32[64,2048]{1,0:T(8,128)S(1)} %get-tuple-element.238, s32[]{:T(128)S(6)} %select_n.10, f32[64,8192]{1,0:T(8,128)S(1)} %get-tuple-element.256, f32[512,8192]{1,0:T(8,128)} %get-tuple-element.223, f32[512]{0:T(512)S(1)} %pmax.12), kind=kOutput, calls=%fused_computation.6.clone.1 | convolution fusion | flops 3225419776 | bytes 19007492 | tf_op jit(solution)/shard_map/while/body/eval_jaxpr/dot_general | solution.py:44
  220.4 9.2 %fusion.25 = (f32[512]{0:T(512)S(1)}, f32[512,8192]{1,0:T(8,128)}) fusion(bf16[64,8192]{1,0:T(8,128)(2,1)} %get-tuple-element.255, bf16[64,2048]{1,0:T(8,128)(2,1)S(1)} %get-tuple-element.253, s32[]{:T(128)S(6)} %select_n.10, f32[8192]{0:T(1024)S(1)} %get-tuple-element.254, f32[512]{0:T(512)S(1)} %multiply_reduce_fusion.4, ...), kind=kOutput, calls=%fused_computation.26.clone.1 | convolution fusion | flops 562036224 | bytes 17960964 | tf_op jit(solution)/shard_map/while/body/eval_jaxpr/dot_general | solution.py:32
  229.6 33.1 %pmax.12 = f32[512]{0:T(512)S(1)} all-reduce(f32[512]{0:T(512)S(1)} %get-tuple-element.224), channel_id=1, replica_groups=mesh['row'=16,'col'=16] {'col'}, use_global_device_ids=true, to_apply=%region_4.0 | all-reduce | flops 512 | bytes 4096 | tf_op jit(solution)/shard_map/while/body/eval_jaxpr/pmax | solution.py:59
  262.8 8.1 %fusion.27 = f32[512]{0:T(512)S(1)} fusion(f32[512,8192]{1,0:T(8,128)} %get-tuple-element.223, f32[512]{0:T(512)S(1)} %pmax.12), kind=kLoop, calls=%fused_computation.2.clone.1 | loop fusion | flops 8388096 | bytes 16781312 | tf_op jit(solution)/shard_map/while/body/eval_jaxpr/reduce_sum | solution.py:43
  270.9 0.3 dynamic_update_slice.18
  271.1 19.6 %fusion.26 = f32[64,2048]{1,0:T(8,128)S(1)} fusion(f32[64,2048]{1,0:T(8,128)S(1)} %get-tuple-element.238, s32[]{:T(128)S(6)} %select_n.10, f32[64,8192]{1,0:T(8,128)S(1)} %get-tuple-element.256, f32[512,8192]{1,0:T(8,128)} %get-tuple-element.223, f32[512]{0:T(512)S(1)} %pmax.12), kind=kOutput, calls=%fused_computation.6.clone.1 | convolution fusion | flops 3225419776 | bytes 19007492 | tf_op jit(solution)/shard_map/while/body/eval_jaxpr/dot_general | solution.py:44
  290.8 9.2 %fusion.25 = (f32[512]{0:T(512)S(1)}, f32[512,8192]{1,0:T(8,128)}) fusion(bf16[64,8192]{1,0:T(8,128)(2,1)} %get-tuple-element.255, bf16[64,2048]{1,0:T(8,128)(2,1)S(1)} %get-tuple-element.253, s32[]{:T(128)S(6)} %select_n.10, f32[8192]{0:T(1024)S(1)} %get-tuple-element.254, f32[512]{0:T(512)S(1)} %multiply_reduce_fusion.4, ...), kind=kOutput, calls=%fused_computation.26.clone.1 | convolution fusion | flops 562036224 | bytes 17960964 | tf_op jit(solution)/shard_map/while/body/eval_jaxpr/dot_general | solution.py:32
  300.0 33.1 %pmax.12 = f32[512]{0:T(512)S(1)} all-reduce(f32[512]{0:T(512)S(1)} %get-tuple-element.224), channel_id=1, replica_groups=mesh['row'=16,'col'=16] {'col'}, use_global_device_ids=true, to_apply=%region_4.0 | all-reduce | flops 512 | bytes 4096 | tf_op jit(solution)/shard_map/while/body/eval_jaxpr/pmax | solution.py:59
  333.1 8.1 %fusion.27 = f32[512]{0:T(512)S(1)} fusion(f32[512,8192]{1,0:T(8,128)} %get-tuple-element.223, f32[512]{0:T(512)S(1)} %pmax.12), kind=kLoop, calls=%fused_computation.2.clone.1 | loop fusion | flops 8388096 | bytes 16781312 | tf_op jit(solution)/shard_map/while/body/eval_jaxpr/reduce_sum | solution.py:43
  341.2 0.3 dynamic_update_slice.18
  341.5 19.6 %fusion.26 = f32[64,2048]{1,0:T(8,128)S(1)} fusion(f32[64,2048]{1,0:T(8,128)S(1)} %get-tuple-element.238, s32[]{:T(128)S(6)} %select_n.10, f32[64,8192]{1,0:T(8,128)S(1)} %get-tuple-element.256, f32[512,8192]{1,0:T(8,128)} %get-tuple-element.223, f32[512]{0:T(512)S(1)} %pmax.12), kind=kOutput, calls=%fused_computation.6.clone.1 | convolution fusion | flops 3225419776 | bytes 19007492 | tf_op jit(solution)/shard_map/while/body/eval_jaxpr/dot_general | solution.py:44
  361.1 0.0 copy-start.1
  361.1 0.8 copy-done.1
  361.9 0.0 reduce-scatter.2.cloned.1.call-update
  361.9 0.0 all-reduce.4.cloned.1.call-start
  362.0 0.0 copy-done.5
  362.0 0.6 dynamic-slice
  363.2 33.8 %all-reduce = f32[2048]{0:T(1024)S(1)} all-reduce(f32[2048]{0:T(1024)S(1)} %get-tuple-element.143), channel_id=3, replica_groups=mesh['row'=16,'col'=16] {'col'}, use_global_device_ids=true, to_apply=%region_8.0.clone | all-reduce | flops 2048 | bytes 16384
  397.0 0.1 dynamic-slice.1
  397.1 38.5 %reduce-scatter.2.cloned.1.call-done = f32[64,128]{1,0:T(8,128)} async-done(((f32[64,2048]{1,0:T(8,128)}), f32[64,128]{1,0:T(8,128)}) %reduce-scatter.2.cloned.1.call-update) | async-done | bytes 32784 | tf_op jit(solution)/shard_map/reduce_scatter | solution.py:64
  435.6 0.8 broadcast_divide_fusion
  436.3 0.0 copy-done
  436.3 0.0 copy-done.3
  436.3 0.0 copy-start.2
  436.4 2.2 fusion.12
  438.6 0.0 copy-done.4
  438.6 2.3 fusion.7
  440.9 0.0 all-reduce.4.cloned.1.call-update
  440.9 0.1 convert_reduce_fusion
  441.0 74.4 %all-reduce.1 = (f32[256]{0:T(256)S(1)}, f32[2000]{0:T(1024)S(1)}, f32[2000]{0:T(1024)S(1)}) all-reduce(f32[256]{0:T(256)S(1)} %convert_reduce_fusion, f32[2000]{0:T(1024)S(1)} %get-tuple-element.145, f32[2000]{0:T(1024)S(1)} %get-tuple-element.144), channel_id=1, replica_groups=mesh['row'=16,'col'=16] {'row','col'}, use_global_device_ids=true, to_apply=%region_13.0 | all-reduce | flops 4256 | bytes 34048 | tf_op jit(solution)/shard_map/psum | solution.py:78
  515.4 189.9 %all-reduce.4.cloned.1.call-done = f32[2000,256]{1,0:T(8,128)} async-done(((f32[2000,256]{1,0:T(8,128)}), f32[2000,256]{1,0:T(8,128)}) %all-reduce.4.cloned.1.call-update) | async-done | bytes 2048016 | tf_op jit(solution)/shard_map/psum | solution.py:78
  705.3 3.5 rsqrt_multiply_fusion
  708.8 0.0 copy-done.2
  (9 shorter events, 0.2 us)
Async XLA Ops:
  7.2 429.2 %copy-start = (f32[64,2000]{1,0:T(8,128)S(1)}, f32[64,2000]{1,0:T(8,128)}, u32[]{:S(2)}) copy-start(f32[64,2000]{1,0:T(8,128)} %param.11) | copy-start | bytes 1536004
  7.2 74.6 %all-gather.3.cloned.1.call-start = ((), (), s32[]{:S(2)}) async-start(), calls=%async_computation.1 | async-start | bytes 1114112 | tf_op jit(solution)/shard_map/all_gather | solution.py:18
  7.9 427.7 %reduce-scatter.2.cloned.1.call-start = ((), (), s32[]{:S(2)}) async-start(), calls=%async_computation.2 | async-start | bytes 557056 | tf_op jit(solution)/shard_map/reduce_scatter | solution.py:64
  84.7 277.2 %copy-start.5 = (u32[256]{0:T(256)S(1)}, u32[256]{0:T(256)}, u32[]{:S(2)}) copy-start(u32[256]{0:T(256)} %constant.74) | copy-start | bytes 3076
  84.7 351.6 %copy-start.3 = (bf16[64,128]{1,0:T(8,128)(2,1)S(1)}, bf16[64,128]{1,0:T(8,128)(2,1)}, u32[]{:S(2)}) copy-start(bf16[64,128]{1,0:T(8,128)(2,1)} %param.7) | copy-start | bytes 49156
  84.8 353.8 %copy-start.4 = (s32[128]{0:T(128)S(1)}, s32[128]{0:T(128)}, u32[]{:S(2)}) copy-start(s32[128]{0:T(128)} %param.10) | copy-start | bytes 1540
  361.1 0.8 copy-start.1
  361.9 343.4 %all-reduce.4.cloned.1.call-start = ((), (), s32[]{:S(2)}) async-start(), calls=%async_computation.3 | async-start | bytes 4096000 | tf_op jit(solution)/shard_map/psum | solution.py:78
  436.3 272.4 %copy-start.2 = (f32[64,128]{1,0:T(8,128)}, f32[64,128]{1,0:T(8,128)S(1)}, u32[]{:S(2)}) copy-start(f32[64,128]{1,0:T(8,128)S(1)} %broadcast_divide_fusion) | copy-start | bytes 98308
Sparse Core Ops, SparseCore 0:
  9.8 72.0 all-gather.2
  362.0 73.4 reduce-scatter.1
  441.6 263.6 all-reduce.3
where the time goes:
time: 716 us; the launch traced here: 715 us
  blocking collectives  293 us (41%)
  waiting for transfers between devices  245 us (34%)
  matrix products  120 us (17%)
  other arithmetic  39.8 us (6%)
  between operations  14.5 us (2%)
    psum x1, waiting for transfers between devices, per_device(): lax.psum((cross_sum, gene_total, gene_square, fate_count), ('row', 'col'))  190 us
    pmax x4, blocking collectives, advance(): row_top = lax.pmax(jnp.max(scores, 1), 'col')  127 us
    dot_general x4, matrix products, accumulate(): lax.dot_general(late_wide, kernel, (((1,), (1,)), ((), ())), precision=pr...  78.4 us
    psum x1, blocking collectives, per_device(): lax.psum((cross_sum, gene_total, gene_square, fate_count), ('row', 'col'))  74.4 us
    reduce_scatter x1, waiting for transfers between devices, per_device(): lax.psum_scatter(numerators, 'col', scatter_dimension=1, tiled=True)  38.5 us
    dot_general x4, matrix products, scores_at(): lax.dot_general(row_slab, late_rows, (((0,), (0,)), ((), ())), preferred_...  36.8 us
    all_gather x1, blocking collectives, per_device(): lax.all_gather(late_log_scale, 'row', axis=0, tiled=True)  36.5 us
    unnamed x1, blocking collectives  33.8 us
  transfers between devices with their start and end apart: 3, of which 3 were waited for; matrix products, arithmetic and copies ran while one was open for 0% of the time, Pallas kernels for 0%

commit v1 on v0

--- a/solution.py
+++ b/solution.py
@@ -76,7 +76,7 @@
     gene_total = jnp.sum(gene_shift, 1)
     gene_square = jnp.sum(gene_shift * gene_shift, 1)
     cross_sum, gene_total, gene_square, fate_count = lax.psum(
-        (cross_sum, gene_total, gene_square, fate_count), ("row", "col")
+        lax.psum((cross_sum, gene_total, gene_square, fate_count), "row"), "col"
     )
     cell_count = float(own_cells * lax.axis_size("row") * col_count)
     mean_shift = gene_total / cell_count

time: 716 us -> 742 us (1.036)
  blocking collectives: 293 us -> 341 us
  waiting for transfers between devices: 245 us -> 219 us
    psum x1 -> x2, blocking collectives: 74.4 us -> 122 us  [the longest x1 62.5 us: per_device(): lax.psum((cross_sum, gene_total, gene_square, fate_count), 'row')]
    psum x1 -> x2, waiting for transfers between devices: 190 us -> 164 us  [the longest x1 142 us: per_device(): lax.psum((cross_sum, gene_total, gene_square, fate_count), 'row')]
  transfers between devices with their start and end apart: 3 -> 4, of which waited for: 3 -> 4; matrix products, arithmetic and copies ran while one was open for 0% -> 0% of each run, Pallas kernels for 0% -> 0%
where the time goes in v1:
time: 742 us; the launch traced here: 736 us
  blocking collectives  341 us (46%)
  waiting for transfers between devices  219 us (30%)
  matrix products  120 us (16%)
  other arithmetic  38.7 us (5%)
  between operations  14.5 us (2%)
    psum x1, waiting for transfers between devices, per_device(): lax.psum((cross_sum, gene_total, gene_square, fate_count), 'row')  142 us
    pmax x4, blocking collectives, advance(): row_top = lax.pmax(jnp.max(scores, 1), 'col')  127 us
    dot_general x4, matrix products, accumulate(): lax.dot_general(late_wide, kernel, (((1,), (1,)), ((), ())), precision=pr...  78.4 us
    psum x1, blocking collectives, per_device(): lax.psum((cross_sum, gene_total, gene_square, fate_count), 'row')  62.5 us
    psum x1, blocking collectives, per_device(): lax.psum(lax.psum((cross_sum, gene_total, gene_square, fate_count), 'row'...  59.7 us
    reduce_scatter x1, waiting for transfers between devices, per_device(): lax.psum_scatter(numerators, 'col', scatter_dimension=1, tiled=True)  38.4 us
    dot_general x4, matrix products, scores_at(): lax.dot_general(row_slab, late_rows, (((0,), (0,)), ((), ())), preferred_...  36.8 us
    all_gather x1, blocking collectives, per_device(): lax.all_gather(late_log_scale, 'row', axis=0, tiled=True)  36.5 us
  transfers between devices with their start and end apart: 4, of which 4 were waited for; matrix products, arithmetic and copies ran while one was open for 0% of the time, Pallas kernels for 0%

profile of v1, /device:TPU:2, one launch (start us, length us, event | category | flops | bytes accessed | tf_op | source)
XLA Modules:
  0.0 736.2 jit_solution(15454384028718442452)
XLA Ops:
  7.2 0.0 copy-start
  7.2 0.0 all-gather.3.cloned.1.call-start
  7.2 0.7 all-gather.3.cloned.1.call-update
  7.9 0.0 reduce-scatter.2.cloned.1.call-start
  8.0 0.7 reshape.14
  8.6 36.5 %all-gather = bf16[16,1,512]{2,1,0:T(2,128)(2,1)S(1)} all-gather(bf16[1,1,512]{2,1,0:T(2,128)(2,1)S(1)} %reshape.14), channel_id=1, replica_groups=mesh['row'=16,'col'=16] {'row'}, dimensions={0}, use_global_device_ids=true | all-gather | bytes 17408 | tf_op jit(solution)/shard_map/all_gather | solution.py:19
  45.2 20.9 %all_gather.10 = bf16[64,2048]{1,0:T(8,128)(2,1)S(1)} all-gather(bf16[64,128]{1,0:T(8,128)(2,1)} %param.7), channel_id=1, replica_groups=mesh['row'=16,'col'=16] {'col'}, dimensions={1}, use_global_device_ids=true | all-gather | bytes 278528 | tf_op jit(solution)/shard_map/all_gather | solution.py:16
  66.1 15.7 %all-gather.3.cloned.1.call-done = bf16[64,8192]{1,0:T(8,128)(2,1)} async-done(((bf16[64,512]{1,0:T(8,128)(2,1)}), bf16[64,8192]{1,0:T(8,128)(2,1)}) %all-gather.3.cloned.1.call-update) | async-done | bytes 1048592 | tf_op jit(solution)/shard_map/all_gather | solution.py:18
  81.8 0.0 copy-start.1
  81.8 1.4 convert_element_type.20
  83.3 0.1 copy-done.1
  83.4 0.3 multiply_reduce_fusion.1
  83.7 0.0 copy-start.6
  83.7 0.0 copy-start.4
  83.7 276.3 %while.15 = (s32[]{:T(128)}, f32[64,2048]{1,0:T(8,128)S(1)}, f32[2048]{0:T(1024)S(1)}, f32[8192]{0:T(1024)S(1)}, bf16[64,2048]{1,0:T(8,128)(2,1)S(1)}, /*index=5...) while((s32[]{:T(128)}, f32[64,2048]{1,0:T(8,128)S(1)}, ...), condition=%wide.region_6.0_spmd, body=%wide.region_1.0_spmd.sunk | while | flops 3795942400 | bytes 53825716 | solution.py:62
  83.8 9.2 %fusion.25 = (f32[512]{0:T(512)S(1)}, f32[512,8192]{1,0:T(8,128)}) fusion(bf16[64,8192]{1,0:T(8,128)(2,1)} %get-tuple-element.258, bf16[64,2048]{1,0:T(8,128)(2,1)S(1)} %get-tuple-element.256, s32[]{:T(128)S(6)} %select_n.10, f32[8192]{0:T(1024)S(1)} %get-tuple-element.257, f32[512]{0:T(512)S(1)} %multiply_reduce_fusion.4, ...), kind=kOutput, calls=%fused_computation.26.clone.1 | convolution fusion | flops 562036224 | bytes 17960964 | tf_op jit(solution)/shard_map/while/body/eval_jaxpr/dot_general | solution.py:32
  93.0 27.9 %pmax.12 = f32[512]{0:T(512)S(1)} all-reduce(f32[512]{0:T(512)S(1)} %get-tuple-element.227), channel_id=1, replica_groups=mesh['row'=16,'col'=16] {'col'}, use_global_device_ids=true, to_apply=%region_4.0 | all-reduce | flops 512 | bytes 4096 | tf_op jit(solution)/shard_map/while/body/eval_jaxpr/pmax | solution.py:59
  120.9 8.1 %fusion.27 = f32[512]{0:T(512)S(1)} fusion(f32[512,8192]{1,0:T(8,128)} %get-tuple-element.226, f32[512]{0:T(512)S(1)} %pmax.12), kind=kLoop, calls=%fused_computation.2.clone.1 | loop fusion | flops 8388096 | bytes 16781312 | tf_op jit(solution)/shard_map/while/body/eval_jaxpr/reduce_sum | solution.py:43
  129.0 0.3 dynamic_update_slice.18
  129.3 19.6 %fusion.26 = f32[64,2048]{1,0:T(8,128)S(1)} fusion(f32[64,2048]{1,0:T(8,128)S(1)} %get-tuple-element.241, s32[]{:T(128)S(6)} %select_n.10, f32[64,8192]{1,0:T(8,128)S(1)} %get-tuple-element.259, f32[512,8192]{1,0:T(8,128)} %get-tuple-element.226, f32[512]{0:T(512)S(1)} %pmax.12), kind=kOutput, calls=%fused_computation.6.clone.1 | convolution fusion | flops 3225419776 | bytes 19007492 | tf_op jit(solution)/shard_map/while/body/eval_jaxpr/dot_general | solution.py:44
  149.0 9.2 %fusion.25 = (f32[512]{0:T(512)S(1)}, f32[512,8192]{1,0:T(8,128)}) fusion(bf16[64,8192]{1,0:T(8,128)(2,1)} %get-tuple-element.258, bf16[64,2048]{1,0:T(8,128)(2,1)S(1)} %get-tuple-element.256, s32[]{:T(128)S(6)} %select_n.10, f32[8192]{0:T(1024)S(1)} %get-tuple-element.257, f32[512]{0:T(512)S(1)} %multiply_reduce_fusion.4, ...), kind=kOutput, calls=%fused_computation.26.clone.1 | convolution fusion | flops 562036224 | bytes 17960964 | tf_op jit(solution)/shard_map/while/body/eval_jaxpr/dot_general | solution.py:32
  158.2 33.1 %pmax.12 = f32[512]{0:T(512)S(1)} all-reduce(f32[512]{0:T(512)S(1)} %get-tuple-element.227), channel_id=1, replica_groups=mesh['row'=16,'col'=16] {'col'}, use_global_device_ids=true, to_apply=%region_4.0 | all-reduce | flops 512 | bytes 4096 | tf_op jit(solution)/shard_map/while/body/eval_jaxpr/pmax | solution.py:59
  191.3 8.1 %fusion.27 = f32[512]{0:T(512)S(1)} fusion(f32[512,8192]{1,0:T(8,128)} %get-tuple-element.226, f32[512]{0:T(512)S(1)} %pmax.12), kind=kLoop, calls=%fused_computation.2.clone.1 | loop fusion | flops 8388096 | bytes 16781312 | tf_op jit(solution)/shard_map/while/body/eval_jaxpr/reduce_sum | solution.py:43
  199.4 0.3 dynamic_update_slice.18
  199.7 19.6 %fusion.26 = f32[64,2048]{1,0:T(8,128)S(1)} fusion(f32[64,2048]{1,0:T(8,128)S(1)} %get-tuple-element.241, s32[]{:T(128)S(6)} %select_n.10, f32[64,8192]{1,0:T(8,128)S(1)} %get-tuple-element.259, f32[512,8192]{1,0:T(8,128)} %get-tuple-element.226, f32[512]{0:T(512)S(1)} %pmax.12), kind=kOutput, calls=%fused_computation.6.clone.1 | convolution fusion | flops 3225419776 | bytes 19007492 | tf_op jit(solution)/shard_map/while/body/eval_jaxpr/dot_general | solution.py:44
  219.4 9.2 %fusion.25 = (f32[512]{0:T(512)S(1)}, f32[512,8192]{1,0:T(8,128)}) fusion(bf16[64,8192]{1,0:T(8,128)(2,1)} %get-tuple-element.258, bf16[64,2048]{1,0:T(8,128)(2,1)S(1)} %get-tuple-element.256, s32[]{:T(128)S(6)} %select_n.10, f32[8192]{0:T(1024)S(1)} %get-tuple-element.257, f32[512]{0:T(512)S(1)} %multiply_reduce_fusion.4, ...), kind=kOutput, calls=%fused_computation.26.clone.1 | convolution fusion | flops 562036224 | bytes 17960964 | tf_op jit(solution)/shard_map/while/body/eval_jaxpr/dot_general | solution.py:32
  228.6 33.1 %pmax.12 = f32[512]{0:T(512)S(1)} all-reduce(f32[512]{0:T(512)S(1)} %get-tuple-element.227), channel_id=1, replica_groups=mesh['row'=16,'col'=16] {'col'}, use_global_device_ids=true, to_apply=%region_4.0 | all-reduce | flops 512 | bytes 4096 | tf_op jit(solution)/shard_map/while/body/eval_jaxpr/pmax | solution.py:59
  261.7 8.1 %fusion.27 = f32[512]{0:T(512)S(1)} fusion(f32[512,8192]{1,0:T(8,128)} %get-tuple-element.226, f32[512]{0:T(512)S(1)} %pmax.12), kind=kLoop, calls=%fused_computation.2.clone.1 | loop fusion | flops 8388096 | bytes 16781312 | tf_op jit(solution)/shard_map/while/body/eval_jaxpr/reduce_sum | solution.py:43
  269.8 0.3 dynamic_update_slice.18
  270.1 19.6 %fusion.26 = f32[64,2048]{1,0:T(8,128)S(1)} fusion(f32[64,2048]{1,0:T(8,128)S(1)} %get-tuple-element.241, s32[]{:T(128)S(6)} %select_n.10, f32[64,8192]{1,0:T(8,128)S(1)} %get-tuple-element.259, f32[512,8192]{1,0:T(8,128)} %get-tuple-element.226, f32[512]{0:T(512)S(1)} %pmax.12), kind=kOutput, calls=%fused_computation.6.clone.1 | convolution fusion | flops 3225419776 | bytes 19007492 | tf_op jit(solution)/shard_map/while/body/eval_jaxpr/dot_general | solution.py:44
  289.7 9.2 %fusion.25 = (f32[512]{0:T(512)S(1)}, f32[512,8192]{1,0:T(8,128)}) fusion(bf16[64,8192]{1,0:T(8,128)(2,1)} %get-tuple-element.258, bf16[64,2048]{1,0:T(8,128)(2,1)S(1)} %get-tuple-element.256, s32[]{:T(128)S(6)} %select_n.10, f32[8192]{0:T(1024)S(1)} %get-tuple-element.257, f32[512]{0:T(512)S(1)} %multiply_reduce_fusion.4, ...), kind=kOutput, calls=%fused_computation.26.clone.1 | convolution fusion | flops 562036224 | bytes 17960964 | tf_op jit(solution)/shard_map/while/body/eval_jaxpr/dot_general | solution.py:32
  298.9 33.1 %pmax.12 = f32[512]{0:T(512)S(1)} all-reduce(f32[512]{0:T(512)S(1)} %get-tuple-element.227), channel_id=1, replica_groups=mesh['row'=16,'col'=16] {'col'}, use_global_device_ids=true, to_apply=%region_4.0 | all-reduce | flops 512 | bytes 4096 | tf_op jit(solution)/shard_map/while/body/eval_jaxpr/pmax | solution.py:59
  332.1 8.1 %fusion.27 = f32[512]{0:T(512)S(1)} fusion(f32[512,8192]{1,0:T(8,128)} %get-tuple-element.226, f32[512]{0:T(512)S(1)} %pmax.12), kind=kLoop, calls=%fused_computation.2.clone.1 | loop fusion | flops 8388096 | bytes 16781312 | tf_op jit(solution)/shard_map/while/body/eval_jaxpr/reduce_sum | solution.py:43
  340.2 0.3 dynamic_update_slice.18
  340.4 19.6 %fusion.26 = f32[64,2048]{1,0:T(8,128)S(1)} fusion(f32[64,2048]{1,0:T(8,128)S(1)} %get-tuple-element.241, s32[]{:T(128)S(6)} %select_n.10, f32[64,8192]{1,0:T(8,128)S(1)} %get-tuple-element.259, f32[512,8192]{1,0:T(8,128)} %get-tuple-element.226, f32[512]{0:T(512)S(1)} %pmax.12), kind=kOutput, calls=%fused_computation.6.clone.1 | convolution fusion | flops 3225419776 | bytes 19007492 | tf_op jit(solution)/shard_map/while/body/eval_jaxpr/dot_general | solution.py:44
  360.0 0.0 copy-start.2
  360.0 0.0 copy-start.5
  360.1 0.8 copy-done.2
  360.8 0.0 reduce-scatter.2.cloned.1.call-update
  360.9 0.0 all-reduce.6.cloned.1.call-start
  360.9 0.0 copy-done.6
  360.9 0.6 dynamic-slice
  362.2 33.8 %all-reduce = f32[2048]{0:T(1024)S(1)} all-reduce(f32[2048]{0:T(1024)S(1)} %get-tuple-element.143), channel_id=3, replica_groups=mesh['row'=16,'col'=16] {'col'}, use_global_device_ids=true, to_apply=%region_8.0.clone | all-reduce | flops 2048 | bytes 16384
  396.0 0.1 dynamic-slice.1
  396.1 38.4 %reduce-scatter.2.cloned.1.call-done = f32[64,128]{1,0:T(8,128)} async-done(((f32[64,2048]{1,0:T(8,128)}), f32[64,128]{1,0:T(8,128)}) %reduce-scatter.2.cloned.1.call-update) | async-done | bytes 32784 | tf_op jit(solution)/shard_map/reduce_scatter | solution.py:64
  434.5 0.8 broadcast_divide_fusion
  435.3 0.0 copy-done
  435.3 0.0 copy-done.4
  435.3 0.0 copy-start.3
  435.3 2.2 fusion.12
  437.5 0.0 copy-done.5
  437.5 2.3 fusion.7
  439.8 0.0 copy-done.3
  439.8 0.0 all-reduce.6.cloned.1.call-update
  439.8 0.0 all-reduce.8.cloned.1.call-start
  439.8 141.8 %all-reduce.6.cloned.1.call-done = f32[2000,256]{1,0:T(8,128)} async-done(((f32[2000,256]{1,0:T(8,128)}), f32[2000,256]{1,0:T(8,128)}) %all-reduce.6.cloned.1.call-update) | async-done | bytes 2048016 | tf_op jit(solution)/shard_map/psum | solution.py:79
  581.6 0.0 all-reduce.8.cloned.1.call-update
  581.6 0.1 convert_reduce_fusion
  581.7 62.5 %all-reduce.2 = (f32[256]{0:T(256)S(1)}, f32[2000]{0:T(1024)S(1)}, f32[2000]{0:T(1024)S(1)}) all-reduce(f32[256]{0:T(256)S(1)} %convert_reduce_fusion, f32[2000]{0:T(1024)S(1)} %get-tuple-element.145, f32[2000]{0:T(1024)S(1)} %get-tuple-element.144), channel_id=1, replica_groups=mesh['row'=16,'col'=16] {'row'}, use_global_device_ids=true, to_apply=%region_15.0 | all-reduce | flops 4256 | bytes 34048 | tf_op jit(solution)/shard_map/psum | solution.py:79
  644.2 59.7 %all-reduce.1 = (f32[256]{0:T(256)S(1)}, f32[2000]{0:T(1024)S(1)}, f32[2000]{0:T(1024)S(1)}) all-reduce(f32[256]{0:T(256)S(1)} %get-tuple-element.165, f32[2000]{0:T(1024)S(1)} %get-tuple-element.166, f32[2000]{0:T(1024)S(1)} %get-tuple-element.167), channel_id=1, replica_groups=mesh['row'=16,'col'=16] {'col'}, use_global_device_ids=true, to_apply=%region_16.0 | all-reduce | flops 4256 | bytes 34048 | tf_op jit(solution)/shard_map/psum | solution.py:78
  704.0 22.2 %all-reduce.8.cloned.1.call-done = f32[2000,256]{1,0:T(8,128)} async-done(((f32[2000,256]{1,0:T(8,128)}), f32[2000,256]{1,0:T(8,128)}) %all-reduce.8.cloned.1.call-update) | async-done | bytes 2048016 | tf_op jit(solution)/shard_map/psum | solution.py:78
  726.2 3.5 rsqrt_multiply_fusion
  (9 shorter events, 0.2 us)
Async XLA Ops:
  7.2 428.1 %copy-start = (f32[64,2000]{1,0:T(8,128)S(1)}, f32[64,2000]{1,0:T(8,128)}, u32[]{:S(2)}) copy-start(f32[64,2000]{1,0:T(8,128)} %param.11) | copy-start | bytes 1536004
  7.2 74.6 %all-gather.3.cloned.1.call-start = ((), (), s32[]{:S(2)}) async-start(), calls=%async_computation.1 | async-start | bytes 1114112 | tf_op jit(solution)/shard_map/all_gather | solution.py:18
  7.9 426.6 %reduce-scatter.2.cloned.1.call-start = ((), (), s32[]{:S(2)}) async-start(), calls=%async_computation.2 | async-start | bytes 557056 | tf_op jit(solution)/shard_map/reduce_scatter | solution.py:64
  81.8 1.5 copy-start.1
  83.7 277.2 %copy-start.6 = (u32[256]{0:T(256)S(1)}, u32[256]{0:T(256)}, u32[]{:S(2)}) copy-start(u32[256]{0:T(256)} %constant.74) | copy-start | bytes 3076
  83.7 351.6 %copy-start.4 = (bf16[64,128]{1,0:T(8,128)(2,1)S(1)}, bf16[64,128]{1,0:T(8,128)(2,1)}, u32[]{:S(2)}) copy-start(bf16[64,128]{1,0:T(8,128)(2,1)} %param.7) | copy-start | bytes 49156
  360.0 0.8 copy-start.2
  360.0 77.4 %copy-start.5 = (s32[128]{0:T(128)S(1)}, s32[128]{0:T(128)}, u32[]{:S(2)}) copy-start(s32[128]{0:T(128)} %param.10) | copy-start | bytes 1540
  360.9 220.8 %all-reduce.6.cloned.1.call-start = ((), (), s32[]{:S(2)}) async-start(), calls=%async_computation.3 | async-start | bytes 4096000 | tf_op jit(solution)/shard_map/psum | solution.py:79
  435.3 4.5 copy-start.3
  439.8 286.4 %all-reduce.8.cloned.1.call-start = ((), (), s32[]{:S(2)}) async-start(), calls=%async_computation.4 | async-start | bytes 4096000 | tf_op jit(solution)/shard_map/psum | solution.py:78
Sparse Core Ops, SparseCore 0:
  9.8 72.0 all-gather.2
  361.0 73.4 reduce-scatter.1
  439.9 141.6 all-reduce.5
  584.1 142.0 all-reduce.7
